TPU v7x, 32 devices: a whole 2x2x4 slice. The times are simulated.
32 devices in a mesh: groups: 2 (over y), inner: 8 (over z, x), outer: 2 (over core).
Axes of the slice: x: 2, y: 2, z: 4, core: 2. Of those that a mesh axis runs over, the one named last changes fastest.
Arguments:
- queries: bfloat16 [4096, 1024], P(('groups', 'outer', 'inner')), parts along dimension 0, may hold values from -6 to 6
- keys: bfloat16 [4096, 2, 1024], P(('groups', 'outer', 'inner')), parts along dimension 0, may hold values from -6 to 6
- values: bfloat16 [4096, 2, 1024], P(('groups', 'outer', 'inner')), parts along dimension 0, may hold values from -6 to 6
- log_gate: float32 [4096, 8], P(('groups', 'outer', 'inner')), parts along dimension 0, may hold values from -1 to 0, as said below
- out_gate: bfloat16 [4096, 1024], P(('groups', 'outer', 'inner')), parts along dimension 0, may hold values from -6 to 6
- norm_gain: float32 [128], replicated, may hold values from 0.1 to 1.9
Outputs:
- gated_output: bfloat16 [4096, 1024], P(('groups', 'outer', 'inner')), parts along dimension 0
There are 2 independent parts, one for each index of `groups`. A program takes and returns all parts, laid end to end along the dimension named above; an argument that names none is the same for every part. Nothing has to cross between parts.
Inputs may be any that keep to these rules, and one draw needn't show every extreme that they name: `log_gate`: logarithm of the factor by which a head's state is scaled at a token; never positive.
All inputs are finite; a program needn't handle non-finite values.
Results may differ from a plain program's by a relative error of at most 0.001.
Values sent between devices are 32-bit elements; how exact they have to be, the bound alone decides.
A program may use at most 512 MiB of HBM per device.

v0:
```python
import jax
import jax.numpy as jnp
from jax import lax
from jax.sharding import PartitionSpec as P

highest = lax.Precision.HIGHEST
eps_norm = 1e-06


def prefix(value, axis, combine, identity):
    size, index = (lax.axis_size(axis), lax.axis_index(axis))
    everything = jax.tree.map(lambda part: lax.all_gather(part, axis), value)
    start = jax.tree.map(
        lambda part, zero: jnp.broadcast_to(jnp.asarray(zero, part.dtype), part.shape),
        value,
        identity,
    )

    def turn(k, before):
        reached = k < index
        new = combine(before, jax.tree.map(lambda part: part[k], everything))
        return jax.tree.map(lambda a, b: jnp.where(reached, a, b), new, before)

    return lax.fori_loop(0, size, turn, start)


def product(pattern, first_op, second_op):
    return jnp.einsum(pattern, first_op, second_op, precision=highest)


def compose(earlier_map, later_map):
    return (
        product("hde,hef->hdf", later_map[0], earlier_map[0]),
        product("hde,hef->hdf", later_map[0], earlier_map[1]) + later_map[1],
    )


def local(queries, keys, values, log_gate, out_gate, norm_gain):
    tok_count = queries.shape[0]
    head_count = log_gate.shape[1]
    head_size = norm_gain.shape[0]
    block_tokens = min(tok_count, 128)
    block_steps = 2 * block_tokens
    block_count = tok_count // block_tokens
    query_blocks = (
        queries.astype(jnp.float32)
        .reshape(block_count, block_tokens, head_count, head_size)
        .transpose(0, 2, 1, 3)
    )
    raw_keys = keys.astype(jnp.float32).reshape(tok_count, 2, head_count, head_size)
    unit_keys = raw_keys * lax.rsqrt(
        jnp.sum(raw_keys * raw_keys, axis=-1, keepdims=True) + eps_norm
    )
    key_blocks = unit_keys.reshape(block_count, block_steps, head_count, head_size).transpose(
        0, 2, 1, 3
    )
    value_blocks = (
        values.astype(jnp.float32)
        .reshape(block_count, block_steps, head_count, head_size)
        .transpose(0, 2, 1, 3)
    )
    step_gate = (
        jnp.stack([log_gate, jnp.zeros_like(log_gate)], axis=1)
        .reshape(block_count, block_steps, head_count)
        .transpose(0, 2, 1)
    )
    row_steps = lax.broadcasted_iota(jnp.int32, (block_steps, block_steps), 0)
    col_steps = lax.broadcasted_iota(jnp.int32, (block_steps, block_steps), 1)
    upper_ones = (row_steps <= col_steps).astype(jnp.float32)
    cumulative = product("bhc,cd->bhd", step_gate, upper_ones)
    strict_lower = row_steps > col_steps
    gaps = cumulative[..., :, None] - cumulative[..., None, :]
    decay_pairs = jnp.where(strict_lower, jnp.exp(jnp.where(strict_lower, gaps, 0.0)), 0.0)
    key_gram = product("bhid,bhjd->bhij", key_blocks, key_blocks)
    system = jnp.eye(block_steps, dtype=jnp.float32) + 2.0 * decay_pairs * key_gram
    growth = jnp.exp(cumulative)
    stacked = jnp.concatenate([value_blocks, growth[..., None] * key_blocks], axis=-1)
    solved = jax.scipy.linalg.solve_triangular(system, stacked, lower=True, unit_diagonal=True)
    base_updates = solved[..., :head_size]
    key_weights = solved[..., head_size:]
    query_cum = cumulative[..., 1::2]
    row_tokens = lax.broadcasted_iota(jnp.int32, (block_tokens, block_steps), 0)
    col_tokens = lax.broadcasted_iota(jnp.int32, (block_tokens, block_steps), 1)
    visible = col_tokens <= 2 * row_tokens + 1
    query_gaps = query_cum[..., :, None] - cumulative[..., None, :]
    query_pairs = jnp.where(visible, jnp.exp(jnp.where(visible, query_gaps, 0.0)), 0.0) * product(
        "bhtd,bhjd->bhtj", query_blocks, key_blocks
    )
    readout = jnp.exp(query_cum)[..., None] * query_blocks - 2.0 * product(
        "bhtj,bhjd->bhtd", query_pairs, key_weights
    )
    local_out = 2.0 * product("bhtj,bhjd->bhtd", query_pairs, base_updates)
    block_growth = growth[..., -1]
    scaled_keys = jnp.exp(cumulative[..., -1:] - cumulative)[..., None] * key_blocks
    eye_states = jnp.broadcast_to(
        jnp.eye(head_size, dtype=jnp.float32), (head_count, head_size, head_size)
    )
    zero_states = jnp.zeros((head_count, head_size, head_size), jnp.float32)
    block_inputs = (block_growth, scaled_keys, key_weights, base_updates, readout, local_out)

    def advance(carried, inputs):
        linear_acc, offset_acc = carried
        grow_now, keys_now, weights_now, updates_now, readout_now, local_now = inputs
        linear_now = grow_now[:, None, None] * eye_states - 2.0 * product(
            "hjd,hje->hde", keys_now, weights_now
        )
        offset_now = 2.0 * product("hjd,hje->hde", keys_now, updates_now)
        emitted = ()
        next_linear = product("hde,hef->hdf", linear_now, linear_acc)
        next_offset = product("hde,hef->hdf", linear_now, offset_acc) + offset_now
        return ((next_linear, next_offset), emitted)

    (device_linear, device_offset), emitted_all = lax.scan(
        advance, (eye_states, zero_states), block_inputs
    )
    joint_before = prefix(
        (device_linear, device_offset), ("outer", "inner"), compose, (eye_states, zero_states)
    )
    incoming = joint_before[1]

    def replay(carried_state, inputs):
        grow_now, keys_now, weights_now, updates_now, readout_now, local_now = inputs
        out_now = product("htd,hde->hte", readout_now, carried_state) + local_now
        change = updates_now - product("hjd,hde->hje", weights_now, carried_state)
        carried_state = grow_now[:, None, None] * carried_state + 2.0 * product(
            "hjd,hje->hde", keys_now, change
        )
        return (carried_state, out_now)

    final_state, head_outputs = lax.scan(replay, incoming, block_inputs)
    head_outputs = head_outputs.transpose(0, 2, 1, 3).reshape(tok_count, head_count, head_size)
    scale_inv = lax.rsqrt(jnp.mean(head_outputs * head_outputs, axis=-1, keepdims=True) + eps_norm)
    gate_vals = jax.nn.silu(out_gate.astype(jnp.float32).reshape(tok_count, head_count, head_size))
    result = head_outputs * scale_inv * norm_gain * gate_vals
    return result.reshape(tok_count, head_count * head_size).astype(jnp.bfloat16)


def solution(mesh):
    in_specs = (
        P(("groups", "outer", "inner"), None),
        P(("groups", "outer", "inner"), None, None),
        P(("groups", "outer", "inner"), None, None),
        P(("groups", "outer", "inner"), None),
        P(("groups", "outer", "inner"), None),
        P(),
    )
    out_specs = P(("groups", "outer", "inner"), None)
    return jax.shard_map(local, mesh=mesh, in_specs=in_specs, out_specs=out_specs, check_vma=False)
```

profile of v0, /device:TPU:27, one launch (start us, length us, event | category | flops | bytes accessed | tf_op | source)
XLA Modules:
  0.0 383.7 jit_solution(2228722775046241144)
XLA Ops:
  13.5 1.6 bitcast_multiply_fusion
  15.1 3.8 select_add_fusion
  19.0 6.0 %while.10 = (s32[]{:T(128)}, f32[8,256,256]{2,1,0:T(8,128)S(1)}, s32[2,2]{1,0:T(2,128)S(1)}, f32[2,8,128,128]{3,2,0,1:T(8,128)}, s32[]{:T(128)}) while((s32[]{:T(128)}, f32[8,256,256]{2,1,0:T(8,128)S(1)}, s32[2,2]{1,0:T(2,128)S(1)}, f32[2,8,128,128]{3,2,0,1:T(8,128)}, s32[]{:T(128)}) %tuple.55), condition=%wide.while_cond, body=%wide.while_body.sunk | while | flops 2 | bytes 1049709 | solution.py:78
  19.8 2.3 bitcast_dynamic-update-slice_fusion.2
  22.7 2.3 bitcast_dynamic-update-slice_fusion.2
  25.0 158.6 %custom-call.4 = f32[8,2,128,128]{2,3,1,0:T(8,128)} custom-call(f32[8,2,128,128]{3,2,1,0:T(8,128)} %bitcast.138), custom_call_target="InvertDiagBlocksLowerTriangular" | custom-call | tf_op jit(solution)/shard_map/jit(_solve_triangular)/vmap()/triangular_solve | solution.py:78
  183.7 1.8 maximum_bitcast_fusion
  189.1 2.6 fusion.11
  192.6 1.4 fusion.35
  194.1 3.0 convolution_multiply_fusion.1
  201.1 2.5 fusion.8
  203.7 2.7 fusion.13
  206.4 2.7 convolution_multiply_fusion
  209.1 58.8 %all-gather.5.cloned.1.call-done = f32[128,128,128]{2,1,0:T(8,128)} async-done(((f32[8,128,128]{2,1,0:T(8,128)}), f32[128,128,128]{2,1,0:T(8,128)}) %all-gather.5.cloned.1.call-update) | async-done | bytes 8388624 | tf_op jit(solution)/shard_map/all_gather | solution.py:12
  267.8 75.4 %all-gather.7.cloned.1.call-done = f32[128,128,128]{2,1,0:T(8,128)} async-done(((f32[8,128,128]{2,1,0:T(8,128)}), f32[128,128,128]{2,1,0:T(8,128)}) %all-gather.7.cloned.1.call-update) | async-done | bytes 8388624 | tf_op jit(solution)/shard_map/all_gather | solution.py:12
  343.2 31.5 %while.11 = (s32[]{:T(128)}, f32[8,128,128]{2,1,0:T(8,128)S(1)}, s32[]{:T(128)}, f32[16,8,128,128]{3,2,1,0:T(8,128)}, f32[16,8,128,128]{3,2,1,0:T(8,128)}, /*index=5*/s32[]{:T(128)}, s32[]{:T(128)}) while((s32[]{:T(128)}, f32[8,128,128]{2,1,0:T(8,128)S(1)}, s32[]{:T(128)}, f32[16,8,128,128]{3,2,1,0:T(8,128)}, ...), condition=%wide.region_2.3_spmd.clone, body=%wide.region_1.2_spmd.clone.sunk | while | flops 201850880 | bytes 3672679 | solution.py:24
  343.3 2.0 fusion.60
  345.3 1.9 fusion.60
  347.3 1.9 fusion.60
  349.2 1.9 fusion.60
  351.2 1.9 fusion.60
  353.2 1.9 fusion.60
  355.1 1.9 fusion.60
  357.1 1.9 fusion.60
  359.1 1.9 fusion.60
  361.0 1.9 fusion.60
  363.0 1.9 fusion.60
  365.0 1.9 fusion.60
  366.9 1.9 fusion.60
  368.9 1.9 fusion.60
  370.9 1.9 fusion.60
  372.8 1.9 fusion.60
  (82 shorter events, 19.4 us)
Async XLA Ops:
  6.5 199.9 %copy-start = (f32[128]{0:T(128)S(1)}, f32[128]{0:T(128)}, u32[]{:S(2)}) copy-start(f32[128]{0:T(128)} %param.13) | copy-start | bytes 1540
  6.5 2.1 copy-start.4
  6.5 261.3 %all-gather.5.cloned.1.call-start = ((), (), s32[]{:S(2)}) async-start(), calls=%async_computation | async-start | bytes 8912896 | tf_op jit(solution)/shard_map/all_gather | solution.py:12
  8.6 185.4 %copy-start.1 = (f32[1,256,8,128]{3,2,1,0:T(8,128)}, f32[1,256,8,128]{3,2,1,0:T(8,128)S(1)}, u32[]{:S(2)}) copy-start(f32[1,256,8,128]{3,2,1,0:T(8,128)S(1)} %reshape.147) | copy-start | bytes 3145732
  8.8 1.5 copy-start.8
  183.7 1.9 copy-start.7
  191.7 0.8 copy-start.2
  194.0 149.2 %all-gather.7.cloned.1.call-start = ((), (), s32[]{:S(2)}) async-start(), calls=%async_computation.1 | async-start | bytes 8912896 | tf_op jit(solution)/shard_map/all_gather | solution.py:12
  194.1 3.0 copy-start.3
  343.2 31.5 %copy-start.5 = (f32[8,128,128]{2,1,0:T(8,128)S(1)}, f32[8,128,128]{2,1,0:T(8,128)}, u32[]{:S(2)}) copy-start(f32[8,128,128]{2,1,0:T(8,128)} %convolution_multiply_fusion) | copy-start | bytes 1572868
  343.2 31.6 %copy-start.6 = (f32[8,128,128]{2,1,0:T(8,128)S(1)}, f32[8,128,128]{2,1,0:T(8,128)}, u32[]{:S(2)}) copy-start(f32[8,128,128]{2,1,0:T(8,128)} %fusion.13) | copy-start | bytes 1572868
Sparse Core Ops, SparseCore 0:
  194.1 73.6 all-gather.4
  270.0 73.1 all-gather.6
where the time goes:
time: 388 us; the launch traced here: 384 us
  other arithmetic  164 us (42%)
  waiting for transfers between devices  134 us (35%)
  matrix products  54.6 us (14%)
  local copies, waits for them, and re-layouts  16.3 us (4%)
  between operations  13.7 us (4%)
    another operation x3, other arithmetic, local(): jax.scipy.linalg.solve_triangular(system, stacked, lower=True, unit_diago...  159 us
    all_gather x2, waiting for transfers between devices, prefix(): everything = jax.tree.map(lambda part: lax.all_gather(part, axis), value)  134 us
    dot_general x26, matrix products, product(): return jnp.einsum(pattern, first_op, second_op, precision=highest)  51.5 us
  transfers between devices with their start and end apart: 2, of which 2 were waited for; matrix products, arithmetic and copies ran while one was open for 4% of the time, Pallas kernels for 0%

commit v1 on v0

v1 whole, which is shorter than its diff:
```python
import jax
import jax.numpy as jnp
from jax import lax
from jax.experimental import pallas as pl
from jax.experimental.pallas import tpu as pltpu
from jax.sharding import PartitionSpec as P

eps_norm = 1e-06
f32 = jnp.float32
bf16 = jnp.bfloat16
MESH = pl.DeviceIdType.MESH
NT = (((1,), (1,)), ((), ()))
TN = (((0,), (0,)), ((), ()))


def mm(a, b):
    return jnp.dot(a, b, preferred_element_type=f32)


def split2(x):
    hi = x.astype(bf16)
    return hi, (x - hi.astype(f32)).astype(bf16)


def split3(x):
    hi, rest = x.astype(bf16), None
    rest = x - hi.astype(f32)
    mid = rest.astype(bf16)
    return hi, mid, (rest - mid.astype(f32)).astype(bf16)


def wide(x):
    return jnp.concatenate(split2(x), axis=1)


def square(x):
    row = jnp.concatenate(split2(x), axis=1)
    return jnp.concatenate([row, row], axis=0)


def mm4(a_wide, b_square, size):
    both = mm(a_wide, b_square)
    return both[:, :size] + both[:, size:]


def local_kernel(k_ref, v_ref, q_ref, lg_ref, aw_ref, b_ref, r_ref, lo_ref):
    steps = k_ref.shape[0]
    toks = q_ref.shape[0]
    heads = lg_ref.shape[0]
    d = k_ref.shape[1] // heads
    half = steps // 2

    def iotas(r, c):
        return (
            lax.broadcasted_iota(jnp.int32, (r, c), 0),
            lax.broadcasted_iota(jnp.int32, (r, c), 1),
        )

    i_st, j_tk = iotas(steps, toks)
    tri_steps = (j_tk <= i_st // 2).astype(f32).astype(bf16)
    i_tk, j_tk2 = iotas(toks, toks)
    tri_toks = (j_tk2 <= i_tk).astype(f32).astype(bf16)
    lgs = split3(lg_ref[...])

    def nt(a, b):
        return lax.dot_general(a, b, NT, preferred_element_type=f32)

    c_col = sum(nt(tri_steps, p) for p in lgs)
    q_col = sum(nt(tri_toks, p) for p in lgs)
    c_row = sum(nt(p, tri_steps) for p in lgs)
    ii, jj = iotas(steps, steps)
    strict = ii > jj
    it, jt = iotas(toks, steps)
    visible = jt <= 2 * it + 1
    hi_, hj_ = iotas(half, half)
    eye = (hi_ == hj_).astype(f32)
    eye_d = (lax.broadcasted_iota(jnp.int32, (d, d), 0) == lax.broadcasted_iota(jnp.int32, (d, d), 1)).astype(f32)
    ones8 = jnp.ones((8, d), bf16)
    onesd = jnp.ones((d, d), bf16)

    group = 4
    for first in range(0, heads, group):
        hs = list(range(first, first + group))
        ks, lower, ncol, nrow, invs = {}, {}, {}, {}, {}
        for h in hs:
            k = k_ref[:, h * d : (h + 1) * d]
            kf = k.astype(f32)
            sq = split2(kf * kf)
            n_c = lax.rsqrt(sum(mm(p, onesd) for p in sq) + eps_norm)
            n_r = lax.rsqrt(sum(nt(ones8, p) for p in sq) + eps_norm)[:1]
            gram = nt(k, k)
            gap = jnp.where(strict, c_col[:, h : h + 1] - c_row[h : h + 1, :], 0.0)
            n_cc = jnp.concatenate([n_c] * (steps // d), axis=1)
            low = jnp.where(strict, jnp.exp(gap) * gram * (2.0 * n_r) * n_cc, 0.0)
            ks[h], lower[h], ncol[h], nrow[h] = k, low, n_c, n_r
            diag = [low[:half, :half], low[half:, half:]]
            m = (hi_ // 2 == hj_ // 2)
            invs[h] = [eye - jnp.where(m, x, 0.0) for x in diag]
        b = 2
        while b < half:
            m = (hi_ // (2 * b) == hj_ // (2 * b)) & ((hi_ // b) % 2 == 1) & ((hj_ // b) % 2 == 0)
            for h in hs:
                for s in range(2):
                    block = lower[h][s * half : (s + 1) * half, s * half : (s + 1) * half]
                    off = jnp.where(m, block, 0.0)
                    iw = split2(invs[h][s])
                    iww = jnp.concatenate(iw, axis=1)
                    t = mm4(iww, square(off), half)
                    invs[h][s] = invs[h][s] - mm4(wide(t), jnp.concatenate([iww, iww], axis=0), half)
            b *= 2
        for h in hs:
            t = mm4(wide(invs[h][1]), square(lower[h][half:, :half]), half)
            c21 = -mm4(wide(t), square(invs[h][0]), half)
            minv = jnp.concatenate(
                [
                    jnp.concatenate([invs[h][0], jnp.zeros((half, half), f32)], axis=1),
                    jnp.concatenate([c21, invs[h][1]], axis=1),
                ],
                axis=0,
            )
            k = ks[h]
            v = v_ref[:, h * d : (h + 1) * d]
            y = sum(mm(p, v) for p in split2(minv))
            grow = jnp.exp(c_row[h : h + 1, :]) * nrow[h]
            w = sum(mm(p, k) for p in split2(minv * grow))
            last = c_col[steps - 1 :, h : h + 1]
            tail = jnp.exp(last - c_col[:, h : h + 1]) * ncol[h]
            kt = jnp.transpose(k.astype(f32)).astype(bf16)
            yw = jnp.concatenate([tail * y, tail * w], axis=1)
            ba = sum(mm(kt, p) for p in split2(2.0 * yw))
            b_ref[h] = ba[:, :d]
            aw_ref[h] = wide(jnp.exp(last) * eye_d - ba[:, d:])
            q = q_ref[:, h * d : (h + 1) * d]
            qc = q_col[:, h : h + 1]
            qgap = jnp.where(visible, qc - c_row[h : h + 1, :], 0.0)
            pairs = jnp.where(visible, jnp.exp(qgap) * nt(q, k) * (2.0 * nrow[h]), 0.0)
            p_hi, p_lo = split2(pairs)
            x_hi, x_lo = split2(jnp.concatenate([y, w], axis=1))
            px = mm(p_hi, x_hi) + mm(p_lo, x_hi) + mm(p_hi, x_lo)
            lo_ref[h] = px[:, :d]
            r_ref[h] = wide(jnp.exp(qc) * q.astype(f32) - px[:, d:])


def chain_kernel(inner, count, aw_ref, b_ref, r_ref, lo_ref, gate_ref, gain_ref, o_ref,
                 s_in, s_out, send_sem, recv_sem):
    heads, d = b_ref.shape[0], b_ref.shape[1]
    me = lax.axis_index("outer") * inner + lax.axis_index("inner")

    def place(i):
        return {"outer": i // inner, "inner": i % inner}

    barrier = pltpu.get_barrier_semaphore()

    @pl.when(me > 0)
    def _():
        pl.semaphore_signal(barrier, inc=1, device_id=place(me - 1), device_id_type=MESH)

    @pl.when(me < count - 1)
    def _():
        pl.semaphore_wait(barrier, 1)

    def copy(h):
        return pltpu.make_async_remote_copy(
            src_ref=s_out.at[h], dst_ref=s_in.at[h],
            send_sem=send_sem.at[h], recv_sem=recv_sem.at[h],
            device_id=place(me + 1), device_id_type=MESH,
        )

    @pl.when(me == 0)
    def _():
        for h in range(heads):
            s_in[h] = jnp.zeros((d, d), f32)

    for h in range(heads):
        @pl.when(me > 0)
        def _():
            copy(h).wait_recv()

        @pl.when(me < count - 1)
        def _():
            s_out[h] = mm4(aw_ref[h], square(s_in[h]), d) + b_ref[h]
            copy(h).start()

    gain = gain_ref[...]
    for h in range(heads):
        out = mm4(r_ref[h], square(s_in[h]), d) + lo_ref[h]
        scale = lax.rsqrt(jnp.mean(out * out, axis=-1, keepdims=True) + eps_norm)
        g = gate_ref[:, h * d : (h + 1) * d].astype(f32)
        o_ref[:, h * d : (h + 1) * d] = (out * scale * gain * (g / (1.0 + jnp.exp(-g)))).astype(bf16)

    @pl.when(me < count - 1)
    def _():
        for h in range(heads):
            copy(h).wait_send()


def vmem_specs(n):
    return [pl.BlockSpec(memory_space=pltpu.VMEM)] * n


def solution(mesh):
    inner = mesh.shape["inner"]
    count = inner * mesh.shape["outer"]

    def local(queries, keys, values, log_gate, out_gate, norm_gain):
        toks, width = queries.shape
        heads = log_gate.shape[1]
        d = width // heads
        steps = 2 * toks
        mats = jax.ShapeDtypeStruct((heads, d, d), f32)
        wides = jax.ShapeDtypeStruct((heads, d, 2 * d), bf16)
        aw, b, r, lo = pl.pallas_call(
            local_kernel,
            out_shape=(wides, mats, wides, mats),
            in_specs=vmem_specs(4),
            out_specs=tuple(vmem_specs(4)),
            compiler_params=pltpu.CompilerParams(vmem_limit_bytes=48 << 20),
            name="local_maps",
        )(keys.reshape(steps, width), values.reshape(steps, width), queries, log_gate.T)
        return pl.pallas_call(
            lambda *refs: chain_kernel(inner, count, *refs),
            out_shape=jax.ShapeDtypeStruct((toks, width), bf16),
            in_specs=vmem_specs(6),
            out_specs=vmem_specs(1)[0],
            scratch_shapes=[
                pltpu.VMEM((heads, d, d), f32),
                pltpu.VMEM((heads, d, d), f32),
                pltpu.SemaphoreType.DMA((heads,)),
                pltpu.SemaphoreType.DMA((heads,)),
            ],
            compiler_params=pltpu.CompilerParams(collective_id=0, has_side_effects=True),
            name="chain",
        )(aw, b, r, lo, out_gate, norm_gain.reshape(1, d))

    spec = P(("groups", "outer", "inner"), None)
    spec3 = P(("groups", "outer", "inner"), None, None)
    return jax.shard_map(
        local, mesh=mesh, in_specs=(spec, spec3, spec3, spec, spec, P()), out_specs=spec, check_vma=False
    )
```

time: 388 us -> 73.6 us (0.19); the launches traced: 384 us -> 73.4 us
  other arithmetic: 164 us -> 0 us
  waiting for transfers between devices: 134 us -> 0 us
  Pallas kernels: 0 us -> 66.2 us
  matrix products: 54.6 us -> 0 us
  between operations: 13.7 us -> 0.06 us
  local copies, waits for them, and re-layouts: 16.3 us -> 7.08 us
    another operation x3 -> x0, other arithmetic: 159 us -> none  [local(): jax.scipy.linalg.solve_triangular(system, stacked, lower=True, unit_diago...]
    all_gather x2 -> x0, waiting for transfers between devices: 134 us -> none  [prefix(): everything = jax.tree.map(lambda part: lax.all_gather(part, axis), value)]
    pallas_call x0 -> x2, Pallas kernels: none -> 66.2 us  [the longest x1 56.5 us: local(): pl.pallas_call(lambda *refs: chain_kernel(inner, count, *refs), out_shape...]
    dot_general x26 -> x0, matrix products: 51.5 us -> none  [product(): return jnp.einsum(pattern, first_op, second_op, precision=highest)]
    another operation x8 -> x0, local copies, waits for them, and re-layouts: 5.95 us -> none
  transfers between devices with their start and end apart: 2 -> 0, of which waited for: 2 -> 0; matrix products, arithmetic and copies ran while one was open for 4% -> 0% of each run, Pallas kernels for 0% -> 0%
where the time goes in v1:
time: 73.6 us; the launch traced here: 73.4 us
  Pallas kernels  66.2 us (90%)
  local copies, waits for them, and re-layouts  7.08 us (10%)
    pallas_call x1, Pallas kernels, local(): pl.pallas_call(lambda *refs: chain_kernel(inner, count, *refs), out_shape...  56.5 us
    pallas_call x1, Pallas kernels, local(): pl.pallas_call(local_kernel, out_shape=(wides, mats, wides, mats), in_spe...  9.74 us
    unnamed x15, local copies, waits for them, and re-layouts  5.59 us

profile of v1, /device:TPU:27, one launch (start us, length us, event | category | flops | bytes accessed | tf_op | source)
XLA Modules:
  0.0 73.4 jit_solution(4727884137165950999)
XLA Ops:
  0.0 0.0 copy-start.6
  0.0 1.3 %reshape.9.k_ref = bf16[256,1024]{1,0:T(8,128)(2,1)S(1)} reshape(bf16[128,2,1024]{2,1,0:T(2,128)(2,1)} %param.7) | data formatting | bytes 1048576 | tf_op jit(solution)/shard_map/reshape | solution.py:219
  1.3 0.0 copy-done.6
  1.3 0.0 copy-start.4
  1.3 0.0 copy-start.5
  1.3 0.2 reshape.10.v_ref
  1.5 0.7 copy-done.4
  2.3 0.0 copy-done.5
  2.3 9.7 %local_maps.1 = (bf16[8,128,256]{2,1,0:T(8,128)(2,1)S(1)}, f32[8,128,128]{2,1,0:T(8,128)S(1)}, bf16[8,128,256]{2,1,0:T(8,128)(2,1)S(1)}, f32[8,128,128]{2,1,0:T(8,128)S(1)}) custom-call(bf16[256,1024]{1,0:T(8,128)(2,1)S(1)} %reshape.9.k_ref, bf16[256,1024]{1,0:T(8,128)(2,1)S(1)} %reshape.10.v_ref, bf16[128,1024]{1,0:T(8,128)(2,1)S(1)} %copy-done.4, ...), custom_call_target="tpu_custom_call" | custom-call | tf_op jit(solution)/shard_map/local_maps/pallas_call | solution.py:212
  12.0 0.0 copy-start
  12.0 0.8 %copy-done = bf16[8,128,256]{2,1,0:T(8,128)(2,1)} copy-done((bf16[8,128,256]{2,1,0:T(8,128)(2,1)}, bf16[8,128,256]{2,1,0:T(8,128)(2,1)S(1)}, u32[]{:S(2)}) %copy-start) | copy-done | bytes 524312
  12.8 0.0 copy-start.1
  12.8 0.8 %copy-done.1 = f32[8,128,128]{2,1,0:T(8,128)} copy-done((f32[8,128,128]{2,1,0:T(8,128)}, f32[8,128,128]{2,1,0:T(8,128)S(1)}, u32[]{:S(2)}) %copy-start.1) | copy-done | bytes 524312
  13.6 0.0 copy-start.2
  13.6 0.8 %copy-done.2 = bf16[8,128,256]{2,1,0:T(8,128)(2,1)} copy-done((bf16[8,128,256]{2,1,0:T(8,128)(2,1)}, bf16[8,128,256]{2,1,0:T(8,128)(2,1)S(1)}, u32[]{:S(2)}) %copy-start.2) | copy-done | bytes 524312
  14.4 0.0 copy-start.3
  14.4 0.8 %copy-done.3 = f32[8,128,128]{2,1,0:T(8,128)} copy-done((f32[8,128,128]{2,1,0:T(8,128)}, f32[8,128,128]{2,1,0:T(8,128)S(1)}, u32[]{:S(2)}) %copy-start.3) | copy-done | bytes 524312
  15.2 56.5 %chain.1 = bf16[128,1024]{1,0:T(8,128)(2,1)} custom-call(bf16[8,128,256]{2,1,0:T(8,128)(2,1)} %copy-done, f32[8,128,128]{2,1,0:T(8,128)} %copy-done.1, bf16[8,128,256]{2,1,0:T(8,128)(2,1)} %copy-done.2, f32[8,128,128]{2,1,0:T(8,128)} %copy-done.3, bf16[128,1024]{1,0:T(8,128)(2,1)} %refs_4_.1, f32[1,128]{1,0:T(1,128)} %bitcast.3), custom_call_target="tpu_custom_call" | custom-call | tf_op jit(solution)/shard_map/chain/pallas_call | solution.py:220
  71.7 1.7 %copy.8 = bf16[128,1024]{1,0:T(8,128)(2,1)} copy(bf16[128,1024]{1,0:T(8,128)(2,1)} %chain.1) | data formatting | bytes 524288
Async XLA Ops:
  0.0 1.3 %copy-start.6 = (bf16[128,2,1024]{2,1,0:T(2,128)(2,1)S(1)}, bf16[128,2,1024]{2,1,0:T(2,128)(2,1)}, u32[]{:S(2)}) copy-start(bf16[128,2,1024]{2,1,0:T(2,128)(2,1)} %param.8) | copy-start | bytes 1572868
  1.3 1.0 %copy-start.4 = (bf16[128,1024]{1,0:T(8,128)(2,1)S(1)}, bf16[128,1024]{1,0:T(8,128)(2,1)}, u32[]{:S(2)}) copy-start(bf16[128,1024]{1,0:T(8,128)(2,1)} %q_ref.1) | copy-start | bytes 786436
  1.3 0.9 %copy-start.5 = (f32[128,8]{0,1:T(8,128)S(1)}, f32[128,8]{0,1:T(8,128)}, u32[]{:S(2)}) copy-start(f32[128,8]{0,1:T(8,128)} %param.9) | copy-start | bytes 12292
  12.0 0.8 %copy-start = (bf16[8,128,256]{2,1,0:T(8,128)(2,1)}, bf16[8,128,256]{2,1,0:T(8,128)(2,1)S(1)}, u32[]{:S(2)}) copy-start(bf16[8,128,256]{2,1,0:T(8,128)(2,1)S(1)} %get-tuple-element.9.refs_0_) | copy-start | bytes 1572868
  12.8 0.8 %copy-start.1 = (f32[8,128,128]{2,1,0:T(8,128)}, f32[8,128,128]{2,1,0:T(8,128)S(1)}, u32[]{:S(2)}) copy-start(f32[8,128,128]{2,1,0:T(8,128)S(1)} %get-tuple-element.10.refs_1_) | copy-start | bytes 1572868
  13.6 0.8 %copy-start.2 = (bf16[8,128,256]{2,1,0:T(8,128)(2,1)}, bf16[8,128,256]{2,1,0:T(8,128)(2,1)S(1)}, u32[]{:S(2)}) copy-start(bf16[8,128,256]{2,1,0:T(8,128)(2,1)S(1)} %get-tuple-element.11.refs_2_) | copy-start | bytes 1572868
  14.4 0.8 %copy-start.3 = (f32[8,128,128]{2,1,0:T(8,128)}, f32[8,128,128]{2,1,0:T(8,128)S(1)}, u32[]{:S(2)}) copy-start(f32[8,128,128]{2,1,0:T(8,128)S(1)} %get-tuple-element.12.refs_3_) | copy-start | bytes 1572868

commit v2 on v1

v2 whole, which is shorter than its diff:
```python
import jax
import jax.numpy as jnp
from jax import lax
from jax.experimental import pallas as pl
from jax.experimental.pallas import tpu as pltpu
from jax.sharding import PartitionSpec as P

eps_norm = 1e-06
f32 = jnp.float32
bf16 = jnp.bfloat16
MESH = pl.DeviceIdType.MESH
NT = (((1,), (1,)), ((), ()))
TN = (((0,), (0,)), ((), ()))


def mm(a, b):
    return jnp.dot(a, b, preferred_element_type=f32)


def split2(x):
    hi = x.astype(bf16)
    return hi, (x - hi.astype(f32)).astype(bf16)


def split3(x):
    hi, rest = x.astype(bf16), None
    rest = x - hi.astype(f32)
    mid = rest.astype(bf16)
    return hi, mid, (rest - mid.astype(f32)).astype(bf16)


def wide(x):
    return jnp.concatenate(split2(x), axis=1)


def square(x):
    row = jnp.concatenate(split2(x), axis=1)
    return jnp.concatenate([row, row], axis=0)


def mm4(a_wide, b_square, size):
    both = mm(a_wide, b_square)
    return both[:, :size] + both[:, size:]


def square_t(x):
    hi, lo = split2(x)
    return jnp.concatenate(
        [jnp.concatenate([hi, hi], axis=1), jnp.concatenate([lo, lo], axis=1)], axis=0
    )


def iotas(r, c):
    return (
        lax.broadcasted_iota(jnp.int32, (r, c), 0),
        lax.broadcasted_iota(jnp.int32, (r, c), 1),
    )


def nt(a, b):
    return lax.dot_general(a, b, NT, preferred_element_type=f32)


def kernel(inner, count, k_ref, v_ref, q_ref, lg_ref, gate_ref, gain_ref, o_ref,
           maps, whole_sq, whole_b, first_sq, r_ref, lo_ref, s_in, s_out, states,
           pair_send, pair_recv, chain_send, chain_recv, state_send, state_recv):
    steps = k_ref.shape[0]
    toks = q_ref.shape[0]
    heads = lg_ref.shape[0]
    d = k_ref.shape[1] // heads
    half = steps // 2
    kept = heads // 2
    parts = chain_send.shape[1]
    rows = d // parts

    me = lax.axis_index("outer") * inner + lax.axis_index("inner")
    par = me % 2
    mate = me + 1 - 2 * par
    has_next = me < count - 2

    def place(i):
        return {"outer": i // inner, "inner": i % inner}

    barrier = pltpu.get_barrier_semaphore()
    pl.semaphore_signal(barrier, inc=1, device_id=place(mate), device_id_type=MESH)

    @pl.when(me >= 2)
    def _():
        pl.semaphore_signal(barrier, inc=1, device_id=place(me - 2), device_id_type=MESH)

    def remote(src, dst, send, recv, target):
        return pltpu.make_async_remote_copy(
            src_ref=src, dst_ref=dst, send_sem=send, recv_sem=recv,
            device_id=place(target), device_id_type=MESH,
        )

    def pair_copy(i):
        h = i + kept * par
        return remote(maps.at[par, h], maps.at[par, h], pair_send.at[i], pair_recv.at[i], mate)

    def chain_copy(i, c):
        piece = pl.ds(c * rows, rows)
        return remote(s_out.at[i, piece], s_in.at[0, i, piece],
                      chain_send.at[i, c], chain_recv.at[i, c], me + 2)

    def state_copy(i):
        return remote(s_in.at[1 - par, i], states.at[i], state_send.at[i], state_recv.at[i], mate)

    i_st, j_tk = iotas(steps, toks)
    tri_steps = (j_tk <= i_st // 2).astype(f32).astype(bf16)
    i_tk, j_tk2 = iotas(toks, toks)
    tri_toks = (j_tk2 <= i_tk).astype(f32).astype(bf16)
    lgs = split3(lg_ref[...])
    c_col = sum(nt(tri_steps, p) for p in lgs)
    q_col = sum(nt(tri_toks, p) for p in lgs)
    c_row = sum(nt(p, tri_steps) for p in lgs)
    ii, jj = iotas(steps, steps)
    strict = ii > jj
    it, jt = iotas(toks, steps)
    visible = jt <= 2 * it + 1
    hi_, hj_ = iotas(half, half)
    eye = (hi_ == hj_).astype(f32)
    di, dj = iotas(d, d)
    eye_d = (di == dj).astype(f32)
    ones8 = jnp.ones((8, d), bf16)
    onesd = jnp.ones((d, d), bf16)

    ks, nrow, solved = {}, {}, {}
    quarter = kept // 2
    for turn in range(2):
        hs = [turn * quarter + x for x in range(quarter)]
        hs = hs + [kept + x for x in hs]
        lower, ncol, invs = {}, {}, {}
        for h in hs:
            k = k_ref[:, h * d : (h + 1) * d]
            kf = k.astype(f32)
            sq = split2(kf * kf)
            n_c = lax.rsqrt(sum(mm(p, onesd) for p in sq) + eps_norm)
            n_r = lax.rsqrt(sum(nt(ones8, p) for p in sq) + eps_norm)[:1]
            gram = nt(k, k)
            gap = jnp.where(strict, c_col[:, h : h + 1] - c_row[h : h + 1, :], 0.0)
            n_cc = jnp.concatenate([n_c] * (steps // d), axis=1)
            low = jnp.where(strict, jnp.exp(gap) * gram * (2.0 * n_r) * n_cc, 0.0)
            ks[h], lower[h], ncol[h], nrow[h] = k, low, n_c, n_r
            diag = [low[:half, :half], low[half:, half:]]
            m = hi_ // 2 == hj_ // 2
            invs[h] = [eye - jnp.where(m, x, 0.0) for x in diag]
        b = 2
        while b < half:
            m = (hi_ // (2 * b) == hj_ // (2 * b)) & ((hi_ // b) % 2 == 1) & ((hj_ // b) % 2 == 0)
            for h in hs:
                for s in range(2):
                    block = lower[h][s * half : (s + 1) * half, s * half : (s + 1) * half]
                    off = jnp.where(m, block, 0.0)
                    iww = wide(invs[h][s])
                    t = mm4(iww, square(off), half)
                    invs[h][s] = invs[h][s] - mm4(wide(t), jnp.concatenate([iww, iww], axis=0), half)
            b *= 2
        for h in hs:
            t = mm4(wide(invs[h][1]), square(lower[h][half:, :half]), half)
            c21 = -mm4(wide(t), square(invs[h][0]), half)
            minv = jnp.concatenate(
                [
                    jnp.concatenate([invs[h][0], jnp.zeros((half, half), f32)], axis=1),
                    jnp.concatenate([c21, invs[h][1]], axis=1),
                ],
                axis=0,
            )
            k = ks[h]
            v = v_ref[:, h * d : (h + 1) * d]
            y = sum(mm(p, v) for p in split2(minv))
            grow = jnp.exp(c_row[h : h + 1, :]) * nrow[h]
            w = sum(mm(p, k) for p in split2(minv * grow))
            last = c_col[steps - 1 :, h : h + 1]
            tail = jnp.exp(last - c_col[:, h : h + 1]) * (2.0 * ncol[h])
            kt = jnp.transpose(k.astype(f32)).astype(bf16)
            wy = jnp.concatenate([tail * w, tail * y], axis=1)
            ab = jnp.transpose(sum(mm(kt, p) for p in split2(wy)))
            maps[par, h] = jnp.concatenate([jnp.exp(last) * eye_d - ab[:d], ab[d:]], axis=0)
            solved[h] = (y, w)
        if turn == 0:
            @pl.when(has_next)
            def _():
                pl.semaphore_wait(barrier, 2)

            @pl.when(me >= count - 2)
            def _():
                pl.semaphore_wait(barrier, 1)
        for i in range(turn * quarter, (turn + 1) * quarter):
            pair_copy(i).start()

    for h in range(heads):
        k = ks[h]
        y, w = solved[h]
        q = q_ref[:, h * d : (h + 1) * d]
        qc = q_col[:, h : h + 1]
        qgap = jnp.where(visible, qc - c_row[h : h + 1, :], 0.0)
        pairs = jnp.where(visible, jnp.exp(qgap) * nt(q, k) * (2.0 * nrow[h]), 0.0)
        p_hi, p_lo = split2(pairs)
        x_hi, x_lo = split2(jnp.concatenate([y, w], axis=1))
        px = mm(p_hi, x_hi) + mm(p_lo, x_hi) + mm(p_hi, x_lo)
        lo_ref[h] = px[:, :d]
        r_ref[h] = wide(jnp.exp(qc) * q.astype(f32) - px[:, d:])

    @pl.when(me < 2)
    def _():
        for i in range(kept):
            s_in[0, i] = jnp.zeros((d, d), f32)

    mine = kept * (1 - par)
    for i in range(kept):
        pair_copy(i).wait_recv()
        at_later = square(maps[1, mine + i, :d])
        both = mm4(wide(maps[0, mine + i]), at_later, d)
        whole_sq[i] = square(both[:d])
        whole_b[i] = both[d:] + maps[1, mine + i, d:]
        first_sq[i] = square(maps[0, mine + i, :d])

    for i in range(kept):
        for c in range(parts):
            lo, hi = c * rows, (c + 1) * rows

            @pl.when((me >= 2) & has_next)
            def _():
                chain_copy(i, c).wait_recv()

            @pl.when(has_next)
            def _():
                s_out[i, lo:hi] = mm4(wide(s_in[0, i, lo:hi]), whole_sq[i], d) + whole_b[i, lo:hi]
                chain_copy(i, c).start()

    gain = gain_ref[...]

    def readout(h, state_t):
        both = nt(r_ref[h], square_t(state_t))
        out = both[:, :d] + both[:, d:] + lo_ref[h]
        scale = lax.rsqrt(jnp.mean(out * out, axis=-1, keepdims=True) + eps_norm)
        cols = pl.ds(pl.multiple_of(h * d, d), d)
        g = gate_ref[:, cols].astype(f32)
        o_ref[:, cols] = (out * scale * gain * (g / (1.0 + jnp.exp(-g)))).astype(bf16)

    for i in range(kept):
        @pl.when((me >= 2) & (me >= count - 2))
        def _():
            for c in range(parts):
                chain_copy(i, c).wait_recv()

        s_in[1, i] = mm4(wide(s_in[0, i]), first_sq[i], d) + maps[0, mine + i, d:]
        state_copy(i).start()
    for i in range(kept):
        readout(mine + i, s_in[par, i])
    for i in range(kept):
        state_copy(i).wait_recv()
        readout(kept * par + i, states[i])

    for i in range(kept):
        pair_copy(i).wait_send()
        state_copy(i).wait_send()

    @pl.when(has_next)
    def _():
        for i in range(kept):
            for c in range(parts):
                chain_copy(i, c).wait_send()


def vmem_specs(n):
    return [pl.BlockSpec(memory_space=pltpu.VMEM)] * n


def solution(mesh):
    inner = mesh.shape["inner"]
    count = inner * mesh.shape["outer"]
    assert inner % 2 == 0

    def local(queries, keys, values, log_gate, out_gate, norm_gain):
        toks, width = queries.shape
        heads = log_gate.shape[1]
        d = width // heads
        steps = 2 * toks
        kept = heads // 2
        parts = 2
        dma = pltpu.SemaphoreType.DMA
        return pl.pallas_call(
            lambda *refs: kernel(inner, count, *refs),
            out_shape=jax.ShapeDtypeStruct((toks, width), bf16),
            in_specs=vmem_specs(6),
            out_specs=vmem_specs(1)[0],
            scratch_shapes=[
                pltpu.VMEM((2, heads, 2 * d, d), f32),
                pltpu.VMEM((kept, 2 * d, 2 * d), bf16),
                pltpu.VMEM((kept, d, d), f32),
                pltpu.VMEM((kept, 2 * d, 2 * d), bf16),
                pltpu.VMEM((heads, d, 2 * d), bf16),
                pltpu.VMEM((heads, d, d), f32),
                pltpu.VMEM((2, kept, d, d), f32),
                pltpu.VMEM((kept, d, d), f32),
                pltpu.VMEM((kept, d, d), f32),
                dma((kept,)), dma((kept,)), dma((kept, parts)), dma((kept, parts)), dma((kept,)), dma((kept,)),
            ],
            compiler_params=pltpu.CompilerParams(
                collective_id=0, has_side_effects=True, vmem_limit_bytes=48 << 20
            ),
            name="delta_product",
        )(keys.reshape(steps, width), values.reshape(steps, width), queries, log_gate.T,
          out_gate, norm_gain.reshape(1, d))

    spec = P(("groups", "outer", "inner"), None)
    spec3 = P(("groups", "outer", "inner"), None, None)
    return jax.shard_map(
        local, mesh=mesh, in_specs=(spec, spec3, spec3, spec, spec, P()), out_specs=spec, check_vma=False
    )
```

time: 73.6 us -> 45 us (0.61)
  Pallas kernels: 66.2 us -> 41.1 us
  local copies, waits for them, and re-layouts: 7.08 us -> 3 us
    pallas_call x2 -> x1, Pallas kernels: 66.2 us -> 41.1 us  [local(): pl.pallas_call(lambda *refs: kernel(inner, count, *refs), out_shape=jax.S...]
    unnamed x15 -> x11, local copies, waits for them, and re-layouts: 5.59 us -> 1.51 us
where the time goes in v2:
time: 45 us; the launch traced here: 44.2 us
  Pallas kernels  41.1 us (91%)
  local copies, waits for them, and re-layouts  3 us (7%)
    pallas_call x1, Pallas kernels, local(): pl.pallas_call(lambda *refs: kernel(inner, count, *refs), out_shape=jax.S...  41.1 us
    unnamed x11, local copies, waits for them, and re-layouts  1.51 us
    reshape x1, local copies, waits for them, and re-layouts, local(): keys.reshape(steps, width)  1.3 us

profile of v2, /device:TPU:27, one launch (start us, length us, event | category | flops | bytes accessed | tf_op | source)
XLA Modules:
  0.0 44.2 jit_solution(2340752108414952157)
XLA Ops:
  0.0 0.0 copy-start.4
  0.0 1.3 %reshape.9.refs_0_ = bf16[256,1024]{1,0:T(8,128)(2,1)S(1)} reshape(bf16[128,2,1024]{2,1,0:T(2,128)(2,1)} %param.7) | data formatting | bytes 1048576 | tf_op jit(solution)/shard_map/reshape | solution.py:305
  1.3 0.0 copy-done.4
  1.3 0.0 copy-start
  1.3 0.0 copy-start.1
  1.3 0.0 copy-start.2
  1.4 0.0 copy-start.3
  1.4 0.2 reshape.10.refs_1_
  1.6 0.7 %copy-done = bf16[128,1024]{1,0:T(8,128)(2,1)S(1)} copy-done((bf16[128,1024]{1,0:T(8,128)(2,1)S(1)}, bf16[128,1024]{1,0:T(8,128)(2,1)}, u32[]{:S(2)}) %copy-start) | copy-done | bytes 262168
  2.3 0.1 copy-done.1
  2.3 0.0 copy-done.2
  2.4 0.0 copy-done.3
  2.4 41.1 %delta_product.1 = bf16[128,1024]{1,0:T(8,128)(2,1)S(1)} custom-call(bf16[256,1024]{1,0:T(8,128)(2,1)S(1)} %reshape.9.refs_0_, bf16[256,1024]{1,0:T(8,128)(2,1)S(1)} %reshape.10.refs_1_, bf16[128,1024]{1,0:T(8,128)(2,1)S(1)} %copy-done, f32[8,128]{1,0:T(8,128)S(1)} %bitcast.2, bf16[128,1024]{1,0:T(8,128)(2,1)S(1)} %copy-done.1, f32[1,128]{1,0:T(1,128)S(1)} %bitcast.3), custom_call_target="tpu_custom_call" | custom-call | tf_op jit(solution)/shard_map/delta_product/pallas_call | solution.py:284
  43.5 0.7 %copy.8 = bf16[128,1024]{1,0:T(8,128)(2,1)} copy(bf16[128,1024]{1,0:T(8,128)(2,1)S(1)} %delta_product.1) | data formatting | bytes 524288
Async XLA Ops:
  0.0 1.3 %copy-start.4 = (bf16[128,2,1024]{2,1,0:T(2,128)(2,1)S(1)}, bf16[128,2,1024]{2,1,0:T(2,128)(2,1)}, u32[]{:S(2)}) copy-start(bf16[128,2,1024]{2,1,0:T(2,128)(2,1)} %param.8) | copy-start | bytes 1572868
  1.3 1.0 %copy-start = (bf16[128,1024]{1,0:T(8,128)(2,1)S(1)}, bf16[128,1024]{1,0:T(8,128)(2,1)}, u32[]{:S(2)}) copy-start(bf16[128,1024]{1,0:T(8,128)(2,1)} %refs_2_.1) | copy-start | bytes 786436
  1.3 1.0 %copy-start.1 = (bf16[128,1024]{1,0:T(8,128)(2,1)S(1)}, bf16[128,1024]{1,0:T(8,128)(2,1)}, u32[]{:S(2)}) copy-start(bf16[128,1024]{1,0:T(8,128)(2,1)} %refs_4_.1) | copy-start | bytes 786436
  1.3 1.0 %copy-start.2 = (f32[128,8]{0,1:T(8,128)S(1)}, f32[128,8]{0,1:T(8,128)}, u32[]{:S(2)}) copy-start(f32[128,8]{0,1:T(8,128)} %param.9) | copy-start | bytes 12292
  1.4 1.0 %copy-start.3 = (f32[128]{0:T(128)S(1)}, f32[128]{0:T(128)}, u32[]{:S(2)}) copy-start(f32[128]{0:T(128)} %param.11) | copy-start | bytes 1540

commit v3 on v2

--- a/solution.py
+++ b/solution.py
@@ -77,6 +77,7 @@
     par = me % 2
     mate = me + 1 - 2 * par
     has_next = me < count - 2
+    early = me < inner
 
     def place(i):
         return {"outer": i // inner, "inner": i % inner}
@@ -186,8 +187,41 @@
             @pl.when(me >= count - 2)
             def _():
                 pl.semaphore_wait(barrier, 1)
-        for i in range(turn * quarter, (turn + 1) * quarter):
-            pair_copy(i).start()
+
+        @pl.when(early)
+        def _():
+            for i in range(turn * quarter, (turn + 1) * quarter):
+                pair_copy(i).start()
+
+    mine = kept * (1 - par)
+
+    def merge(i):
+        pair_copy(i).wait_recv()
+        at_later = square(maps[1, mine + i, :d])
+        both = mm4(wide(maps[0, mine + i]), at_later, d)
+        whole_sq[i] = square(both[:d])
+        whole_b[i] = both[d:] + maps[1, mine + i, d:]
+        first_sq[i] = square(maps[0, mine + i, :d])
+
+    @pl.when(me < 2)
+    def _():
+        for i in range(kept):
+            s_in[0, i] = jnp.zeros((d, d), f32)
+
+    def forward(i, c):
+        lo, hi = c * rows, (c + 1) * rows
+        s_out[i, lo:hi] = mm4(wide(s_in[0, i, lo:hi]), whole_sq[i], d) + whole_b[i, lo:hi]
+        chain_copy(i, c).start()
+
+    @pl.when(early)
+    def _():
+        for i in range(quarter):
+            merge(i)
+
+            @pl.when((me < 2) & has_next)
+            def _():
+                for c in range(parts):
+                    forward(i, c)
 
     for h in range(heads):
         k = ks[h]
@@ -202,32 +236,27 @@
         lo_ref[h] = px[:, :d]
         r_ref[h] = wide(jnp.exp(qc) * q.astype(f32) - px[:, d:])
 
-    @pl.when(me < 2)
+    @pl.when(jnp.logical_not(early))
     def _():
         for i in range(kept):
-            s_in[0, i] = jnp.zeros((d, d), f32)
-
-    mine = kept * (1 - par)
-    for i in range(kept):
-        pair_copy(i).wait_recv()
-        at_later = square(maps[1, mine + i, :d])
-        both = mm4(wide(maps[0, mine + i]), at_later, d)
-        whole_sq[i] = square(both[:d])
-        whole_b[i] = both[d:] + maps[1, mine + i, d:]
-        first_sq[i] = square(maps[0, mine + i, :d])
-
-    for i in range(kept):
-        for c in range(parts):
-            lo, hi = c * rows, (c + 1) * rows
-
-            @pl.when((me >= 2) & has_next)
-            def _():
+            pair_copy(i).start()
+        for i in range(quarter):
+            merge(i)
+
+    for i in range(quarter, kept):
+        merge(i)
+
+        @pl.when((me < 2) & has_next)
+        def _():
+            for c in range(parts):
+                forward(i, c)
+
+    @pl.when((me >= 2) & has_next)
+    def _():
+        for i in range(kept):
+            for c in range(parts):
                 chain_copy(i, c).wait_recv()
-
-            @pl.when(has_next)
-            def _():
-                s_out[i, lo:hi] = mm4(wide(s_in[0, i, lo:hi]), whole_sq[i], d) + whole_b[i, lo:hi]
-                chain_copy(i, c).start()
+                forward(i, c)
 
     gain = gain_ref[...]
 
@@ -247,7 +276,6 @@
 
         s_in[1, i] = mm4(wide(s_in[0, i]), first_sq[i], d) + maps[0, mine + i, d:]
         state_copy(i).start()
-    for i in range(kept):
         readout(mine + i, s_in[par, i])
     for i in range(kept):
         state_copy(i).wait_recv()

time: 45 us -> 41.9 us (0.931)
  Pallas kernels: 41.1 us -> 38 us
    pallas_call x1, Pallas kernels: 41.1 us -> 38 us  [local(): pl.pallas_call(lambda *refs: kernel(inner, count, *refs), out_shape=jax.S...]
where the time goes in v3:
time: 41.9 us; the launch traced here: 41.1 us
  Pallas kernels  38 us (91%)
  local copies, waits for them, and re-layouts  3 us (7%)
    pallas_call x1, Pallas kernels, local(): pl.pallas_call(lambda *refs: kernel(inner, count, *refs), out_shape=jax.S...  38 us
    unnamed x11, local copies, waits for them, and re-layouts  1.51 us
    reshape x1, local copies, waits for them, and re-layouts, local(): keys.reshape(steps, width)  1.3 us

profile of v3, /device:TPU:27, one launch (start us, length us, event | category | flops | bytes accessed | tf_op | source)
XLA Modules:
  0.0 41.1 jit_solution(7855804388974571911)
XLA Ops:
  0.0 0.0 copy-start.4
  0.0 1.3 %reshape.9.refs_0_ = bf16[256,1024]{1,0:T(8,128)(2,1)S(1)} reshape(bf16[128,2,1024]{2,1,0:T(2,128)(2,1)} %param.7) | data formatting | bytes 1048576 | tf_op jit(solution)/shard_map/reshape | solution.py:333
  1.3 0.0 copy-done.4
  1.3 0.0 copy-start
  1.3 0.0 copy-start.1
  1.3 0.0 copy-start.2
  1.4 0.0 copy-start.3
  1.4 0.2 reshape.10.refs_1_
  1.6 0.7 %copy-done = bf16[128,1024]{1,0:T(8,128)(2,1)S(1)} copy-done((bf16[128,1024]{1,0:T(8,128)(2,1)S(1)}, bf16[128,1024]{1,0:T(8,128)(2,1)}, u32[]{:S(2)}) %copy-start) | copy-done | bytes 262168
  2.3 0.1 copy-done.1
  2.3 0.0 copy-done.2
  2.4 0.0 copy-done.3
  2.4 38.0 %delta_product.1 = bf16[128,1024]{1,0:T(8,128)(2,1)S(1)} custom-call(bf16[256,1024]{1,0:T(8,128)(2,1)S(1)} %reshape.9.refs_0_, bf16[256,1024]{1,0:T(8,128)(2,1)S(1)} %reshape.10.refs_1_, bf16[128,1024]{1,0:T(8,128)(2,1)S(1)} %copy-done, f32[8,128]{1,0:T(8,128)S(1)} %bitcast.2, bf16[128,1024]{1,0:T(8,128)(2,1)S(1)} %copy-done.1, f32[1,128]{1,0:T(1,128)S(1)} %bitcast.3), custom_call_target="tpu_custom_call" | custom-call | tf_op jit(solution)/shard_map/delta_product/pallas_call | solution.py:312
  40.4 0.7 %copy.8 = bf16[128,1024]{1,0:T(8,128)(2,1)} copy(bf16[128,1024]{1,0:T(8,128)(2,1)S(1)} %delta_product.1) | data formatting | bytes 524288
Async XLA Ops:
  0.0 1.3 %copy-start.4 = (bf16[128,2,1024]{2,1,0:T(2,128)(2,1)S(1)}, bf16[128,2,1024]{2,1,0:T(2,128)(2,1)}, u32[]{:S(2)}) copy-start(bf16[128,2,1024]{2,1,0:T(2,128)(2,1)} %param.8) | copy-start | bytes 1572868
  1.3 1.0 %copy-start = (bf16[128,1024]{1,0:T(8,128)(2,1)S(1)}, bf16[128,1024]{1,0:T(8,128)(2,1)}, u32[]{:S(2)}) copy-start(bf16[128,1024]{1,0:T(8,128)(2,1)} %refs_2_.1) | copy-start | bytes 786436
  1.3 1.0 %copy-start.1 = (bf16[128,1024]{1,0:T(8,128)(2,1)S(1)}, bf16[128,1024]{1,0:T(8,128)(2,1)}, u32[]{:S(2)}) copy-start(bf16[128,1024]{1,0:T(8,128)(2,1)} %refs_4_.1) | copy-start | bytes 786436
  1.3 1.0 %copy-start.2 = (f32[128,8]{0,1:T(8,128)S(1)}, f32[128,8]{0,1:T(8,128)}, u32[]{:S(2)}) copy-start(f32[128,8]{0,1:T(8,128)} %param.9) | copy-start | bytes 12292
  1.4 1.0 %copy-start.3 = (f32[128]{0:T(128)S(1)}, f32[128]{0:T(128)}, u32[]{:S(2)}) copy-start(f32[128]{0:T(128)} %param.11) | copy-start | bytes 1540
